TPU v7x, 256 devices: a whole 4x4x8 slice. The times are simulated.
256 devices in a mesh: gy: 32 (over z, y), gz: 8 (over x, core).
Axes of the slice: x: 4, y: 4, z: 8, core: 2. Of those that a mesh axis runs over, the one named last changes fastest.
Arguments:
- wavefunction: float32 [2, 8, 4096, 2048], P(None, None, 'gy', 'gz'), may hold values from -6 to 6
- absorber: float32 [8, 4096, 2048], P(None, 'gy', 'gz'), may hold values from 0.05 to 1.5
- row_inverse: float32 [2, 4096, 128], P(None, 'gy'), may hold values from -1 to 1
- column_inverse: float32 [2, 2048, 256], replicated, may hold values from -1 to 1
- link_terms: float32 [2, 2, 2], replicated, may hold values from 0.65 to 0.7
- shell_blocks: int32 [8, 32, 56], P('gz'), may hold values from 0 to 63, as said below
- owner_map: int32 [8, 32, 56, 1], P('gz'), may hold values from 0 to 31; in each aligned block of 56 rows (0 to 55, 56 to 111, ..., all dimensions but the last counted through in order) at most 4 rows name the same one
- volkov_phase: float32 [128, 128], replicated, may hold values from -3.140625 to 3.140625
Outputs:
- damped: float32 [2, 8, 4096, 2048], P(None, None, 'gy', 'gz')
- spectrum: float32 [2, 256, 1024, 128], P(None, 'gy', 'gz')
Inputs may be any that keep to these rules, and one draw needn't show every extreme that they name: `shell_blocks`: the ids listed for one device are distinct. `owner_map`: at most 4 of one device's listed blocks name the same owner.
All inputs are finite; a program needn't handle non-finite values.
Results may differ from a plain program's by a relative error of at most 0.0003.
Values sent between devices are 32-bit elements; how exact they have to be, the bound alone decides.
A program may use at most 64 MiB of HBM per device.

v0:
```python
import math

import jax
import jax.numpy as jnp
import numpy as np
from jax import lax
from jax.experimental import pallas as pl
from jax.experimental.pallas import tpu as pltpu
from jax.sharding import PartitionSpec as P

MESH = pl.DeviceIdType.MESH
BF = jnp.bfloat16
F32 = jnp.float32

NX = 8
CY = 128
CZ = 256
K = 128
BY = 2
CAP = 4
NG = 32
NC = 8
UNITS = 16
CHUNKS = 2
PER = NX // CHUNKS


def split(value):
    high = value.astype(BF)
    return high, (value - high.astype(F32)).astype(BF)


NN = (((1,), (0,)), ((), ()))
NT = (((1,), (1,)), ((), ()))


def dot(a, b, dims=NN):
    return lax.dot_general(a, b, dims, preferred_element_type=F32)


def dot3(ah, al, bh, bl, dims=NN):
    return dot(ah, bh, dims) + dot(ah, bl, dims) + dot(al, bh, dims)


def cmul(a, b):
    return (a[0] * b[0] - a[1] * b[1], a[0] * b[1] + a[1] * b[0])


def cadd(a, b):
    return (a[0] + b[0], a[1] + b[1])


def chain(count, stride, edges_of, keep, result):
    lane = lax.broadcasted_iota(jnp.int32, (1, 128), 1)

    def units(j):
        one = lambda i: (lane == stride * j + i).astype(F32)
        return (one(0), one(1)), (one(2), one(3))

    def forward(j, carry):
        coupling, carried = (carry[0], carry[1]), (carry[2], carry[3])
        lead_left, tail_left, lead_right, tail_right = edges_of(j)
        head, tail = units(j)
        step = cmul(lead_left, coupling)
        pivot = (1.0 - step[0], -step[1])
        modulus = pivot[0] * pivot[0] + pivot[1] * pivot[1]
        inverse = (pivot[0] / modulus, -pivot[1] / modulus)
        gain = cmul(tail_left, inverse)
        keep[j, 0:1, :] = coupling[0]
        keep[j, 1:2, :] = coupling[1]
        keep[j, 2:3, :] = carried[0]
        keep[j, 3:4, :] = carried[1]
        keep[j, 4:5, :] = inverse[0]
        keep[j, 5:6, :] = inverse[1]
        after = cadd(tail_right, cmul(gain, cmul(lead_right, coupling)))
        held = cadd(cmul(gain, carried), cadd(tail, cmul(cmul(gain, coupling), head)))
        return (after[0], after[1], held[0], held[1])

    zero = jnp.zeros((1, 128), F32)
    lax.fori_loop(0, count, forward, (zero, zero, zero, zero))

    def backward(k, carry):
        j = count - 1 - k
        following = (carry[0], carry[1])
        lead_left, _, lead_right, _ = edges_of(j)
        head, _ = units(j)
        coupling = (keep[j, 0:1, :], keep[j, 1:2, :])
        carried = (keep[j, 2:3, :], keep[j, 3:4, :])
        inverse = (keep[j, 4:5, :], keep[j, 5:6, :])
        offset = cmul(cadd(head, cmul(lead_left, carried)), inverse)
        value = cadd(offset, cmul(cmul(lead_right, inverse), following))
        left = cadd(carried, cmul(coupling, value))
        result[j, 0:1, :] = left[0]
        result[j, 1:2, :] = left[1]
        result[j, 2:3, :] = following[0]
        result[j, 3:4, :] = following[1]
        return value

    lax.fori_loop(0, count, backward, (zero, zero))


def kernel(
    links,
    slots,
    wave_hbm,
    absorber_hbm,
    row_hbm,
    column_hbm,
    place_row,
    volkov,
    etab,
    ftab,
    damped_hbm,
    spectrum_hbm,
    wave,
    absorber,
    row,
    column,
    top,
    bottom,
    yemb,
    yedge32,
    yedge,
    spikes,
    psi,
    edge_tile,
    edges,
    heads,
    gathered,
    keep,
    response,
    flat_a,
    flat_v,
    values_out,
    values_in,
    solved,
    field,
    zemb,
    zedge32,
    zedge,
    zheads,
    zall,
    zkeep,
    zresponse,
    square,
    zspike,
    zfix,
    solved_z,
    damped,
    fold,
    blocks,
    outgoing,
    incoming,
    ytab,
    spectrum,
    load_sem,
    store_sem,
    edge_sem,
    head_sem,
    value_sem,
    z_sem,
    block_send,
    block_recv,
):
    me = lax.axis_index("gy")
    mez = lax.axis_index("gz")
    half = me // UNITS
    base = half * UNITS
    unit = me - base

    def load(number, source, target):
        copy = pltpu.make_async_copy(source, target, load_sem.at[number])
        copy.start()
        return copy

    row_load = load(0, row_hbm, row)
    wave_load = load(1, wave_hbm, wave)
    column_load = load(2, column_hbm.at[:, mez], column)
    top_load = load(3, column_hbm.at[:, :, pl.ds(0, 8), :], top)
    bottom_load = load(4, column_hbm.at[:, :, pl.ds(CZ - 8, 8), :], bottom)
    absorber_load = load(5, absorber_hbm, absorber)

    barrier = pltpu.get_barrier_semaphore()

    def greet(s, carry):
        pl.semaphore_signal(
            barrier, inc=1, device_id={"gy": lax.rem(me + s, NG)}, device_id_type=MESH
        )
        return carry

    def greet_z(s, carry):
        pl.semaphore_signal(
            barrier, inc=1, device_id={"gz": lax.rem(mez + s, NC)}, device_id_type=MESH
        )
        return carry

    lax.fori_loop(1, NG, greet, 0)
    lax.fori_loop(1, NC, greet_z, 0)

    row_load.wait()
    yr, yi = row[0], row[1]
    for part, (value, sign) in enumerate(((yr, 1.0), (yi, 1.0))):
        high, low = split(value)
        for n, piece in enumerate((high, low)):
            if part == 0:
                yemb[n, 0:CY, 0:CY] = piece
                yemb[n, CY:, CY:] = piece
            else:
                yemb[n, 0:CY, CY:] = -piece
                yemb[n, CY:, 0:CY] = piece
    yedge32[...] = jnp.zeros_like(yedge32)
    for n, r in enumerate((0, CY - 1)):
        yedge32[2 * n : 2 * n + 1, 0:CY] = row[0, r : r + 1, :]
        yedge32[2 * n : 2 * n + 1, CY:] = -row[1, r : r + 1, :]
        yedge32[2 * n + 1 : 2 * n + 2, 0:CY] = row[1, r : r + 1, :]
        yedge32[2 * n + 1 : 2 * n + 2, CY:] = row[0, r : r + 1, :]
    high, low = split(yedge32[...])
    yedge[0], yedge[1] = high, low

    for side, place in enumerate((0, CY - 1)):
        link = (links[2 * side], links[2 * side + 1])
        spike = cmul(link, (yr[:, place : place + 1], yi[:, place : place + 1]))
        for part in range(2):
            spikes[2 * side + part] = jnp.broadcast_to(spike[part], (CY, 128))
            for n, r in enumerate((0, CY - 1)):
                edge_tile[4 * side + 2 * n + part : 4 * side + 2 * n + part + 1, :] = (
                    spikes[2 * side + part, r : r + 1, :]
                )

    pl.semaphore_wait(barrier, NG - 1 + NC - 1)

    def send_edges(s, carry):
        pltpu.make_async_remote_copy(
            src_ref=edge_tile,
            dst_ref=edges.at[me],
            send_sem=edge_sem.at[0],
            recv_sem=edge_sem.at[1],
            device_id={"gy": lax.rem(me + s, NG)},
            device_id_type=MESH,
        ).start()
        return carry

    lax.fori_loop(1, NG, send_edges, 0)
    edges[me] = edge_tile[...]

    wave_load.wait()

    def head_step(x, carry):
        value = jnp.concatenate([wave[0, x], wave[1, x]], axis=0)
        high, low = split(value)
        psi[0, x], psi[1, x] = high, low
        found = dot3(yedge[0], yedge[1], high, low)
        heads[2 * x] = found[0:4, 0:128]
        heads[2 * x + 1] = found[0:4, 128:256]
        return carry

    lax.fori_loop(0, NX, head_step, 0, unroll=True)

    def send_heads(s, carry):
        peer = lax.rem(me + s, NG)
        pltpu.make_async_remote_copy(
            src_ref=heads.at[lax.rem(peer, UNITS)],
            dst_ref=gathered.at[me],
            send_sem=head_sem.at[0],
            recv_sem=head_sem.at[1],
            device_id={"gy": peer},
            device_id_type=MESH,
        ).start()
        return carry

    lax.fori_loop(1, NG, send_heads, 0)
    gathered[me] = heads[unit]

    pltpu.make_async_copy(edges.at[pl.ds(0, NG - 1)], edges.at[pl.ds(0, NG - 1)], edge_sem.at[1]).wait()

    def row_edges(j):
        return [
            (edges[j, r : r + 1, :], edges[j, r + 1 : r + 2, :]) for r in (0, 2, 4, 6)
        ]

    chain(NG, 4, row_edges, keep, response)
    for j in range(NG):
        flat_a[4 * j : 4 * j + 4, :] = response[j]

    def solve_step(x, carry):
        solved[x] = dot3(yemb[0], yemb[1], psi[0, x], psi[1, x])
        return carry

    lax.fori_loop(0, NX, solve_step, 0, unroll=True)

    pltpu.make_async_copy(
        gathered.at[pl.ds(0, NG - 1)], gathered.at[pl.ds(0, NG - 1)], head_sem.at[1]
    ).wait()
    for j in range(NG):
        flat_v[4 * j : 4 * j + 4, :] = gathered[j]
    ah, al = split(flat_a[...])
    vh, vl = split(flat_v[...])
    found = dot3(ah, al, vh, vl)
    for j in range(NG):
        values_out[j] = found[4 * j : 4 * j + 4, :]

    def send_values(s, carry):
        peer = base + lax.rem(unit + s, UNITS)
        pltpu.make_async_remote_copy(
            src_ref=values_out.at[peer],
            dst_ref=values_in.at[unit],
            send_sem=value_sem.at[0],
            recv_sem=value_sem.at[1],
            device_id={"gy": peer},
            device_id_type=MESH,
        ).start()
        return carry

    lax.fori_loop(1, UNITS, send_values, 0)
    values_in[unit] = values_out[me]

    column_load.wait()
    for part in range(2):
        for n, piece in enumerate(split(column[part])):
            if part == 0:
                zemb[n, 0:CZ, 0:CZ] = piece
                zemb[n, CZ:, CZ:] = piece
            else:
                zemb[n, 0:CZ, CZ:] = -piece
                zemb[n, CZ:, 0:CZ] = piece
    zedge32[...] = jnp.zeros_like(zedge32)
    for n, r in enumerate((0, CZ - 1)):
        zedge32[2 * n : 2 * n + 1, 0:CZ] = column[0, r : r + 1, :]
        zedge32[2 * n : 2 * n + 1, CZ:] = -column[1, r : r + 1, :]
        zedge32[2 * n + 1 : 2 * n + 2, 0:CZ] = column[1, r : r + 1, :]
        zedge32[2 * n + 1 : 2 * n + 2, CZ:] = column[0, r : r + 1, :]
    high, low = split(zedge32[...])
    zedge[0], zedge[1] = high, low

    for side in range(2):
        link = (links[4 + 2 * side], links[5 + 2 * side])
        lines = []
        for part in range(2):
            pieces = []
            for a in range(2):
                turned = jnp.transpose(
                    column[part, 128 * a : 128 * a + 128, 128 * side : 128 * side + 128]
                )
                pieces.append(turned[0:1, :] if side == 0 else turned[127:128, :])
            lines.append(jnp.concatenate(pieces, axis=1))
        spike = cmul(link, (lines[0], lines[1]))
        zspike[2 * side : 2 * side + 1, 0:CZ] = spike[0]
        zspike[2 * side : 2 * side + 1, CZ:] = spike[1]
        zspike[2 * side + 1 : 2 * side + 2, 0:CZ] = -spike[1]
        zspike[2 * side + 1 : 2 * side + 2, CZ:] = spike[0]

    top_load.wait()
    bottom_load.wait()

    def column_edges(c):
        out = []
        for side, place in enumerate((0, CZ - 1)):
            link = (links[4 + 2 * side], links[5 + 2 * side])
            for table, r in ((top, 0), (bottom, 7)):
                value = tuple(
                    jnp.broadcast_to(table[part, c, r : r + 1, place : place + 1], (1, 128))
                    for part in range(2)
                )
                out.append(cmul(link, value))
        return out

    chain(NC, 8, column_edges, zkeep, zresponse)
    square[...] = jnp.zeros_like(square)
    square[0:4, :] = zresponse[mez]
    turned = jnp.transpose(square[...])
    for h in range(2):
        total = jnp.zeros((64, 2 * CZ), F32)
        for i in range(4):
            total = total + turned[0:64, i : i + 1] * zspike[i : i + 1, :]
        if h == 0:
            held = total
        else:
            held = pltpu.roll(held, 4, 0)
        high, low = split(held)
        zfix[h, 0:64, :] = high
        zfix[h, 64:128, :] = high
        zfix[h, 128:192, :] = low
        zfix[h, 192:256, :] = low

    wanted = lax.broadcasted_iota(jnp.int32, (2 * K, 16 * NG), 0)
    onehot = (wanted == place_row[...]).astype(F32).astype(BF)
    for n in range(2):
        ytab[n] = dot(etab[n], onehot).astype(BF)

    pltpu.make_async_copy(
        values_in.at[pl.ds(0, UNITS - 1)], values_in.at[pl.ds(0, UNITS - 1)], value_sem.at[1]
    ).wait()

    def field_step(x, carry):
        for h in range(2):
            v = values_in[2 * x + h]
            lre, lim, rre, rim = (v[i : i + 1, :] for i in range(4))
            re = solved[x, 0:CY, 128 * h : 128 * h + 128]
            im = solved[x, CY:, 128 * h : 128 * h + 128]
            re = re + (spikes[0] * lre - spikes[1] * lim) + (spikes[2] * rre - spikes[3] * rim)
            im = im + (spikes[0] * lim + spikes[1] * lre) + (spikes[2] * rim + spikes[3] * rre)
            for part, value in enumerate((re, im)):
                high, low = split(value)
                at = CZ * part + 128 * h
                field[0, x, :, at : at + 128] = high
                field[1, x, :, at : at + 128] = low
        return carry

    lax.fori_loop(0, NX, field_step, 0)

    for x in range(NX):
        found = dot3(zedge[0], zedge[1], field[0, x], field[1, x], NT)
        at = 4 * (x // 4)
        zheads[at : at + 4, 128 * (x % 4) : 128 * (x % 4) + 128] = found[0:4, :]

    def send_zheads(s, carry):
        pltpu.make_async_remote_copy(
            src_ref=zheads,
            dst_ref=zall.at[mez],
            send_sem=z_sem.at[0],
            recv_sem=z_sem.at[1],
            device_id={"gz": lax.rem(mez + s, NC)},
            device_id_type=MESH,
        ).start()
        return carry

    lax.fori_loop(1, NC, send_zheads, 0)
    zall[mez] = zheads[...]

    def solve_z(x, carry):
        solved_z[x] = dot3(field[0, x], field[1, x], zemb[0], zemb[1], NT)
        return carry

    lax.fori_loop(0, NX, solve_z, 0, unroll=True)
    absorber_load.wait()

    pltpu.make_async_copy(
        zall.at[pl.ds(0, NC - 1)], zall.at[pl.ds(0, NC - 1)], z_sem.at[1]
    ).wait()

    for part in range(CHUNKS):
        for x in range(PER * part, PER * part + PER):
            lanes = 128 * (x % 4)
            g = zall[:, :, lanes : lanes + 128].reshape(8 * NC, 128)
            high = g.astype(BF).astype(F32)
            turned = jnp.transpose(jnp.concatenate([high, g - high], axis=0)).astype(BF)
            fix = dot(jnp.concatenate([turned, turned], axis=1), zfix[x // 4])
            kept = jnp.exp(-absorber[x])
            for c in range(2):
                value = solved_z[x, :, CZ * c : CZ * c + CZ] + fix[:, CZ * c : CZ * c + CZ]
                left = value * kept
                damped[c, x] = left
                lost = value - left
                fold[c] = lost[:, 0:128] + lost[:, 128:256]
                for b in range(BY):
                    blocks[x, pl.ds(2 * c + b, K // BY, stride=4), :] = fold[
                        c, pl.ds(b, K // BY, stride=BY), :
                    ]

        def pack(o, carry):
            for l in range(CAP):
                at = slots[CAP * o + l]
                for x in range(PER * part, PER * part + PER):
                    outgoing[x, o, 4 * l : 4 * l + 4, :] = blocks[x, pl.ds(at, 4), :]
            return carry

        lax.fori_loop(0, NG, pack, 0)

        def send_blocks(s, carry):
            peer = lax.rem(me + s, NG)
            pltpu.make_async_remote_copy(
                src_ref=outgoing.at[pl.ds(PER * part, PER), peer],
                dst_ref=incoming.at[pl.ds(PER * part, PER), me],
                send_sem=block_send.at[part],
                recv_sem=block_recv.at[part],
                device_id={"gy": peer},
                device_id_type=MESH,
            ).start()
            return carry

        lax.fori_loop(1, NG, send_blocks, 0)
        for x in range(PER * part, PER * part + PER):
            incoming[x, me] = outgoing[x, me]

    damped_store = pltpu.make_async_copy(damped, damped_hbm, store_sem.at[0])
    damped_store.start()
    norm = 1.0 / math.sqrt(CY * CZ)

    stores = []
    for part in range(CHUNKS):
        pltpu.make_async_copy(
            incoming.at[pl.ds(PER * part, PER), pl.ds(0, NG - 1)],
            incoming.at[pl.ds(PER * part, PER), pl.ds(0, NG - 1)],
            block_recv.at[part],
        ).wait()
        for x in range(PER * part, PER * part + PER):
            high, low = split(incoming[x].reshape(16 * NG, 128))
            along_y = dot3(ytab[0], ytab[1], high, low)
            high, low = split(jnp.concatenate([along_y[0:K, :], along_y[K:, :]], axis=1))
            both = dot3(high, low, ftab[0], ftab[1])
            re, im = cmul((volkov[0], volkov[1]), (both[:, 0:K], both[:, K:]))
            spectrum[0, x] = re * norm
            spectrum[1, x] = im * norm
        store = pltpu.make_async_copy(
            spectrum.at[:, pl.ds(PER * part, PER)],
            spectrum_hbm.at[:, pl.ds(PER * part, PER)],
            store_sem.at[1 + part],
        )
        store.start()
        stores.append(store)

    def sent(ref, count, sem):
        view = ref.at[pl.ds(0, count)]
        pltpu.make_async_copy(view, view, sem).wait()

    sent(edges, NG - 1, edge_sem.at[0])
    sent(gathered, NG - 1, head_sem.at[0])
    sent(values_in, UNITS - 1, value_sem.at[0])
    sent(zall, NC - 1, z_sem.at[0])
    for part in range(CHUNKS):
        view = outgoing.at[pl.ds(PER * part, PER), pl.ds(0, NG - 1)]
        pltpu.make_async_copy(view, view, block_send.at[part]).wait()
    damped_store.wait()
    for store in stores:
        store.wait()


def phase_tables():
    n, k = np.arange(K)[:, None], np.arange(K)[None, :]
    angle = 2.0 * np.pi / K * ((n * k) % K) - np.pi * (n % 2)
    re, im = np.cos(angle), -np.sin(angle)
    along_y = np.block([[re.T, -im.T], [im.T, re.T]]).astype(np.float32)
    along_z = np.block([[re, im], [-im, re]]).astype(np.float32)
    found = []
    for table in (along_y, along_z):
        high = table.astype(BF)
        found.append(np.stack([high, (table - high.astype(np.float32)).astype(BF)]))
    return found


def body(
    wavefunction,
    absorber,
    row_inverse,
    column_inverse,
    link_terms,
    shell_blocks,
    owner_map,
    volkov_phase,
):
    row_rank = lax.axis_index("gy")
    listed, targets = shell_blocks[0], owner_map[0, :, :, 0]
    count = listed.shape[1]
    places = jnp.arange(count, dtype=jnp.int32)
    earlier = places[:, None] > places[None, :]
    rank = jnp.sum(
        ((targets[:, :, None] == targets[:, None, :]) & earlier[None]).astype(jnp.int32), axis=2
    )
    own = lambda table: lax.dynamic_index_in_dim(table, row_rank, 0, keepdims=False)
    slot = own(targets) * CAP + own(rank)
    numbers = jnp.arange(NG * CAP, dtype=jnp.int32)
    first = 2 * BY * own(listed)[None, :]
    slots = jnp.sum(jnp.where(slot[None, :] == numbers[:, None], first, 0), axis=1)
    hit = (targets == row_rank)[:, None, :] & (
        rank[:, None, :] == jnp.arange(CAP, dtype=jnp.int32)[None, :, None]
    )
    coming = jnp.sum(jnp.where(hit, listed[:, None, :] + 1, 0), axis=2) - 1
    comp = jnp.arange(2, dtype=jnp.int32)[None, None, :, None]
    b = jnp.arange(BY, dtype=jnp.int32)[None, None, None, :]
    block = coming[:, :, None, None]
    place_row = jnp.where(block >= 0, comp * K + BY * block + b, -1).reshape(1, 16 * NG)
    volkov = jnp.stack([jnp.cos(volkov_phase), jnp.sin(volkov_phase)])
    etab, ftab = phase_tables()

    any_space = pl.BlockSpec(memory_space=pl.ANY)
    vmem = pl.BlockSpec(memory_space=pltpu.VMEM)
    smem = pl.BlockSpec(memory_space=pltpu.SMEM)
    V = pltpu.VMEM
    dma = pltpu.SemaphoreType.DMA
    return pl.pallas_call(
        kernel,
        out_shape=(
            jax.ShapeDtypeStruct((2, NX, CY, CZ), F32),
            jax.ShapeDtypeStruct((2, NX, K, K), F32),
        ),
        in_specs=[smem, smem] + [any_space] * 4 + [vmem] * 4,
        out_specs=(any_space, any_space),
        scratch_shapes=[
            V((2, NX, CY, CZ), F32),
            V((NX, CY, CZ), F32),
            V((2, CY, CY), F32),
            V((2, CZ, CZ), F32),
            V((2, NC, 8, CZ), F32),
            V((2, NC, 8, CZ), F32),
            V((2, 2 * CY, 2 * CY), BF),
            V((16, 2 * CY), F32),
            V((2, 16, 2 * CY), BF),
            V((4, CY, 128), F32),
            V((2, NX, 2 * CY, CZ), BF),
            V((8, 128), F32),
            V((NG, 8, 128), F32),
            V((UNITS, 4, 128), F32),
            V((NG, 4, 128), F32),
            V((NG, 8, 128), F32),
            V((NG, 4, 128), F32),
            V((4 * NG, 128), F32),
            V((4 * NG, 128), F32),
            V((NG, 4, 128), F32),
            V((UNITS, 4, 128), F32),
            V((NX, 2 * CY, CZ), F32),
            V((2, NX, CY, 2 * CZ), BF),
            V((2, 2 * CZ, 2 * CZ), BF),
            V((16, 2 * CZ), F32),
            V((2, 16, 2 * CZ), BF),
            V((8, 512), F32),
            V((NC, 8, 512), F32),
            V((NC, 8, 128), F32),
            V((NC, 4, 128), F32),
            V((128, 128), F32),
            V((4, 2 * CZ), F32),
            V((2, 256, 2 * CZ), BF),
            V((NX, CY, 2 * CZ), F32),
            V((2, NX, CY, CZ), F32),
            V((2, CY, 128), F32),
            V((NX, 2 * CY, 128), F32),
            V((NX, NG, 16, 128), F32),
            V((NX, NG, 16, 128), F32),
            V((2, 2 * K, 16 * NG), BF),
            V((2, NX, K, K), F32),
            dma((6,)),
            dma((1 + CHUNKS,)),
            dma((2,)),
            dma((2,)),
            dma((2,)),
            dma((2,)),
            dma((CHUNKS,)),
            dma((CHUNKS,)),
        ],
        compiler_params=pltpu.CompilerParams(
            collective_id=0, has_side_effects=True, vmem_limit_bytes=48 * 1024 * 1024
        ),
    )(
        link_terms.reshape(8),
        slots,
        wavefunction,
        absorber,
        row_inverse,
        column_inverse.reshape(2, NC, CZ, CZ),
        place_row,
        volkov,
        etab,
        ftab,
    )


def solution(mesh):
    placed = (
        P(None, None, "gy", "gz"),
        P(None, "gy", "gz"),
        P(None, "gy", None),
        P(),
        P(),
        P("gz", None, None),
        P("gz", None, None, None),
        P(),
    )
    return jax.shard_map(
        body,
        mesh=mesh,
        in_specs=placed,
        out_specs=(P(None, None, "gy", "gz"), P(None, "gy", "gz", None)),
        check_vma=False,
    )
```

profile of v0, /device:TPU:24, one launch (start us, length us, event | category | flops | bytes accessed | tf_op | source)
XLA Modules:
  0.0 97.1 jit_solution(1902140962845049566)
XLA Ops:
  0.6 0.8 reshape.120.links
  1.4 0.7 fusion.5
  2.1 0.7 broadcast_compare_fusion
  2.8 1.7 %convert_reduce_fusion = s32[32,56]{1,0:T(8,128)S(1)} fusion(s32[32,56]{1,0:T(8,128)} %bitcast.20, pred[56,56]{1,0:T(8,128)(4,1)S(1)} %iota_compare_fusion.2), kind=kLoop, calls=%fused_computation | loop fusion | flops 399616 | bytes 17472 | tf_op jit(solution)/shard_map/reduce_sum | solution.py:556
  4.5 0.7 fusion.6
  5.2 0.1 select_reduce_fusion.1.slots
  5.3 0.7 add_bitcast_fusion
  6.0 0.1 select_reduce_fusion
  6.2 0.1 copy.12
  6.3 0.1 copy.13
  6.4 0.1 broadcast_add_fusion
  6.5 0.3 add_select_fusion
  6.8 0.2 select_n.32.place_row
  7.0 1.1 %cosine_bitcast_fusion = (f32[1,128,128]{2,1,0:T(8,128)S(1)}, f32[1,128,128]{2,1,0:T(8,128)S(1)}) fusion(f32[128,128]{1,0:T(8,128)} %param.17), kind=kLoop, calls=%fused_computation.4 | loop fusion | bytes 196608 | tf_op jit(solution)/shard_map/stack | solution.py:572
  8.1 0.0 copy-start
  8.1 1.2 %copy-done = f32[8,128,256]{2,1,0:T(8,128)S(1)} copy-done((f32[8,128,256]{2,1,0:T(8,128)S(1)}, f32[8,128,256]{2,1,0:T(8,128)}, u32[]{:S(2)}) %copy-start) | copy-done | bytes 1048600
  9.3 0.9 copy-done.1
  10.3 0.0 copy-start.2
  10.3 0.9 copy-done.2
  11.2 0.0 copy-start.3
  11.2 0.9 copy-done.3
  12.1 82.7 %shard_map.113 = (f32[2,8,128,256]{3,2,1,0:T(8,128)S(1)}, f32[2,8,128,128]{3,2,1,0:T(8,128)S(1)}) custom-call(f32[8]{0:T(128)S(1)} %reshape.120.links, s32[128]{0:T(128)S(1)} %select_reduce_fusion.1.slots, f32[2,8,128,256]{3,2,1,0:T(8,128)} %wave_hbm.1, f32[8,128,256]{2,1,0:T(8,128)S(1)} %copy-done, f32[2,128,128]{2,1,0:T(8,128)S(1)} %copy-done.3, ...), custom_call_target="tpu_custom_call" | custom-call | tf_op jit(solution)/shard_map/pallas_call | solution.py:580
  94.8 1.3 %copy.16 = f32[2,8,128,256]{3,2,1,0:T(8,128)} copy(f32[2,8,128,256]{3,2,1,0:T(8,128)S(1)} %get-tuple-element.6) | data formatting | bytes 4194304
  96.2 1.0 copy.17
  (6 shorter events, 0.0 us)
Async XLA Ops:
  8.1 1.2 %copy-start = (f32[8,128,256]{2,1,0:T(8,128)S(1)}, f32[8,128,256]{2,1,0:T(8,128)}, u32[]{:S(2)}) copy-start(f32[8,128,256]{2,1,0:T(8,128)} %absorber_hbm.1) | copy-start | bytes 3145732
  9.3 0.9 copy-start.1
  10.3 0.9 copy-start.2
  11.2 0.9 copy-start.3
where the time goes:
time: 97.6 us; the launch traced here: 97.1 us
  Pallas kernels  82.7 us (85%)
  local copies, waits for them, and re-layouts  8.53 us (9%)
  other arithmetic  5.19 us (5%)
    pallas_call x1, Pallas kernels, body(): pl.pallas_call(kernel, out_shape=(jax.ShapeDtypeStruct((2, NX, CY, CZ), F...  82.7 us
    unnamed x10, local copies, waits for them, and re-layouts  6.31 us

commit v1 on v0

v1 whole, which is shorter than its diff:
```python
import math

import jax
import jax.numpy as jnp
import numpy as np
from jax import lax
from jax.experimental import pallas as pl
from jax.experimental.pallas import tpu as pltpu
from jax.sharding import PartitionSpec as P

MESH = pl.DeviceIdType.MESH
BF = jnp.bfloat16
F32 = jnp.float32

NX = 8
PAIRS = 4
CY = 128
CZ = 256
K = 128
BY = 2
CAP = 4
SLOT = 2 * BY * CAP
NG = 32
NC = 8
UNITS = 16
PARTS = ((0, 1), (1, 3), (3, 4))


def split(value):
    high = value.astype(BF)
    return high, (value - high.astype(F32)).astype(BF)


NN = (((1,), (0,)), ((), ()))
NT = (((1,), (1,)), ((), ()))


def dot(a, b, dims=NN):
    return lax.dot_general(a, b, dims, preferred_element_type=F32)


def dot3(ah, al, bh, bl, dims=NN):
    return dot(ah, bh, dims) + dot(ah, bl, dims) + dot(al, bh, dims)


def cmul(a, b):
    return (a[0] * b[0] - a[1] * b[1], a[0] * b[1] + a[1] * b[0])


def cadd(a, b):
    return (a[0] + b[0], a[1] + b[1])


def cinv(a):
    modulus = a[0] * a[0] + a[1] * a[1]
    return (a[0] / modulus, -a[1] / modulus)


def chain(count, stride, edges):
    shape = (count, 128)
    place = lax.broadcasted_iota(jnp.int32, shape, 0)
    lane = lax.broadcasted_iota(jnp.int32, shape, 1) - stride * place
    one = jnp.ones(shape, F32)
    zero = jnp.zeros(shape, F32)
    head = ((lane == 0).astype(F32), (lane == 1).astype(F32))
    tail = ((lane == 2).astype(F32), (lane == 3).astype(F32))
    lead_left, tail_left, lead_right, tail_right = edges

    def shifted(value, by, fill):
        if by > 0:
            return jnp.where(place >= by, pltpu.roll(value, by, 0), fill)
        return jnp.where(place < count + by, pltpu.roll(value, count + by, 0), fill)

    def moved(value, by, fill):
        return (shifted(value[0], by, fill), shifted(value[1], by, zero))

    a, b = cmul(tail_left, lead_right), cmul(tail_right, lead_left)
    m = [(a[0] - b[0], a[1] - b[1]), tail_right, (-lead_left[0], -lead_left[1]), (one, zero)]
    by = 1
    while by < count:
        q = [moved(m[0], by, one), moved(m[1], by, zero), moved(m[2], by, zero), moved(m[3], by, one)]
        m = [
            cadd(cmul(m[0], q[0]), cmul(m[1], q[2])),
            cadd(cmul(m[0], q[1]), cmul(m[1], q[3])),
            cadd(cmul(m[2], q[0]), cmul(m[3], q[2])),
            cadd(cmul(m[2], q[1]), cmul(m[3], q[3])),
        ]
        by *= 2
    coupling = cmul(moved(m[1], 1, zero), cinv(moved(m[3], 1, one)))

    def affine(factor, addend, sign):
        by = 1
        while by < count:
            before = (moved(factor, sign * by, one), moved(addend, sign * by, zero))
            addend = cadd(cmul(factor, before[1]), addend)
            factor = cmul(factor, before[0])
            by *= 2
        return addend

    step = cmul(lead_left, coupling)
    inverse = cinv((1.0 - step[0], -step[1]))
    gain = cmul(tail_left, inverse)
    carried = moved(affine(gain, cadd(tail, cmul(cmul(gain, coupling), head)), 1), 1, zero)
    offset = cmul(cadd(head, cmul(lead_left, carried)), inverse)
    value = affine(cmul(lead_right, inverse), offset, -1)
    return cadd(carried, cmul(coupling, value)), moved(value, -1, zero)


def embed(target, size, real, imag):
    for n, piece in enumerate(split(real)):
        target[n, 0:size, 0:size] = piece
        target[n, size:, size:] = piece
    for n, piece in enumerate(split(imag)):
        target[n, 0:size, size:] = -piece
        target[n, size:, 0:size] = piece


def embed_edges(target, wide, size, source):
    wide[...] = jnp.zeros_like(wide)
    for n, r in enumerate((0, size - 1)):
        wide[2 * n : 2 * n + 1, 0:size] = source[0, r : r + 1, :]
        wide[2 * n : 2 * n + 1, size:] = -source[1, r : r + 1, :]
        wide[2 * n + 1 : 2 * n + 2, 0:size] = source[1, r : r + 1, :]
        wide[2 * n + 1 : 2 * n + 2, size:] = source[0, r : r + 1, :]
    target[0], target[1] = split(wide[...])


def rows_of(block):
    k = lax.broadcasted_iota(jnp.int32, (1, SLOT * NG), 1)
    row = (k // BY) % 2 * K + k % BY
    row = jnp.where(block > 0.5, row.astype(F32) + BY * (block - 1.0), -1.0)
    place = lax.broadcasted_iota(jnp.int32, (2 * K, SLOT * NG), 0).astype(F32)
    return (place == row).astype(F32)


def kernel(
    links,
    wave_hbm,
    absorber_hbm,
    row_hbm,
    column_hbm,
    blocks_hbm,
    owners_hbm,
    phase_hbm,
    tables_hbm,
    damped_hbm,
    spectrum_hbm,
    wave,
    absorber,
    row,
    column,
    top,
    bottom,
    listed,
    owners,
    phase,
    tables,
    yemb,
    ywide,
    yedge,
    spikes,
    psi,
    heads,
    gathered,
    edges,
    flat_a,
    flat_v,
    values_out,
    values_in,
    solved,
    field,
    zemb,
    zwide,
    zedge,
    zheads,
    zall,
    zcorner,
    zresponse,
    square,
    zspike,
    zfix,
    padded,
    pick,
    damped,
    outgoing,
    incoming,
    ytab,
    volkov,
    spectrum,
    load_sem,
    damped_sem,
    spectrum_sem,
    head_sem,
    value_sem,
    z_send,
    z_recv,
    block_send,
    block_recv,
):
    me = lax.axis_index("gy")
    mez = lax.axis_index("gz")
    half = me // UNITS
    base = half * UNITS
    unit = me - base

    barrier = pltpu.get_barrier_semaphore()

    def greet(s, carry):
        pl.semaphore_signal(
            barrier, inc=1, device_id={"gy": lax.rem(me + s, NG)}, device_id_type=MESH
        )
        return carry

    def greet_z(s, carry):
        pl.semaphore_signal(
            barrier, inc=1, device_id={"gz": lax.rem(mez + s, NC)}, device_id_type=MESH
        )
        return carry

    def load(number, source, target):
        copy = pltpu.make_async_copy(source, target, load_sem.at[number])
        copy.start()
        return copy

    row_load = load(0, row_hbm, row)
    wave_load = load(1, wave_hbm, wave)
    lax.fori_loop(1, NG, greet, 0)
    lax.fori_loop(1, NC, greet_z, 0)
    column_load = load(2, column_hbm.at[:, mez], column)
    top_load = load(3, column_hbm.at[:, :, pl.ds(0, 8), :], top)
    bottom_load = load(4, column_hbm.at[:, :, pl.ds(CZ - 8, 8), :], bottom)
    blocks_load = load(5, blocks_hbm, listed)
    owners_load = load(6, owners_hbm, owners)
    absorber_load = load(7, absorber_hbm, absorber)
    tables_load = load(8, tables_hbm, tables)
    phase_load = load(9, phase_hbm, phase)

    row_load.wait()
    embed_edges(yedge, ywide, CY, row)
    lane = lax.broadcasted_iota(jnp.int32, (1, 128), 1)
    edge_row = jnp.zeros((1, 128), F32)
    for side, place in enumerate((0, CY - 1)):
        link = (links[0, side, 0], links[0, side, 1])
        spike = cmul(link, (row[0, :, place : place + 1], row[1, :, place : place + 1]))
        for part in range(2):
            spikes[2 * side + part] = jnp.broadcast_to(spike[part], (CY, 128))
            for n, r in enumerate((0, CY - 1)):
                term = spikes[2 * side + part, r : r + 1, :]
                edge_row = jnp.where(lane == 4 * side + 2 * n + part, term, edge_row)
    for u in range(UNITS):
        heads[u, 4] = edge_row

    wave_load.wait()
    for x in range(NX):
        high, low = split(jnp.concatenate([wave[0, x], wave[1, x]], axis=0))
        psi[0, x], psi[1, x] = high, low
        found = dot3(yedge[0], yedge[1], high, low)
        for h in range(2):
            for i in range(4):
                heads[2 * x + h, i] = found[i : i + 1, 128 * h : 128 * h + 128]

    pl.semaphore_wait(barrier, NG - 1 + NC - 1)

    def send_heads(s, carry):
        peer = lax.rem(me + s, NG)
        pltpu.make_async_remote_copy(
            src_ref=heads.at[lax.rem(peer, UNITS)],
            dst_ref=gathered.at[me],
            send_sem=head_sem.at[0],
            recv_sem=head_sem.at[1],
            device_id={"gy": peer},
            device_id_type=MESH,
        ).start()
        return carry

    lax.fori_loop(1, NG, send_heads, 0)
    gathered[me] = heads[unit]

    embed(yemb, CY, row[0], row[1])
    for x in range(NX):
        solved[x] = dot3(yemb[0], yemb[1], psi[0, x], psi[1, x])

    pltpu.make_async_copy(
        gathered.at[pl.ds(0, NG - 1)], gathered.at[pl.ds(0, NG - 1)], head_sem.at[1]
    ).wait()
    for j in range(NG):
        for i in range(4):
            flat_v[4 * j + i : 4 * j + i + 1, :] = gathered[j, i]
        edges[j : j + 1, :] = gathered[j, 4]
    wide = [jnp.broadcast_to(edges[:, i : i + 1], (NG, 128)) for i in range(8)]
    left, right = chain(NG, 4, [(wide[i], wide[i + 1]) for i in (0, 2, 4, 6)])
    for i, value in enumerate(left + right):
        flat_a[pl.ds(i, NG, stride=4), :] = value
    ah, al = split(flat_a[...])
    vh, vl = split(flat_v[...])
    found = dot3(ah, al, vh, vl)
    for j in range(NG):
        values_out[j] = found[4 * j : 4 * j + 4, :]

    def send_values(s, carry):
        peer = base + lax.rem(unit + s, UNITS)
        pltpu.make_async_remote_copy(
            src_ref=values_out.at[peer],
            dst_ref=values_in.at[unit],
            send_sem=value_sem.at[0],
            recv_sem=value_sem.at[1],
            device_id={"gy": peer},
            device_id_type=MESH,
        ).start()
        return carry

    lax.fori_loop(1, UNITS, send_values, 0)
    values_in[unit] = values_out[me]

    column_load.wait()
    embed(zemb, CZ, column[0], column[1])
    embed_edges(zedge, zwide, CZ, column)
    for side in range(2):
        link = (links[1, side, 0], links[1, side, 1])
        lines = []
        for part in range(2):
            pieces = []
            for a in range(2):
                turned = jnp.transpose(
                    column[part, 128 * a : 128 * a + 128, 128 * side : 128 * side + 128]
                )
                pieces.append(turned[0:1, :] if side == 0 else turned[127:128, :])
            lines.append(jnp.concatenate(pieces, axis=1))
        spike = cmul(link, (lines[0], lines[1]))
        zspike[2 * side : 2 * side + 1, 0:CZ] = spike[0]
        zspike[2 * side : 2 * side + 1, CZ:] = spike[1]
        zspike[2 * side + 1 : 2 * side + 2, 0:CZ] = -spike[1]
        zspike[2 * side + 1 : 2 * side + 2, CZ:] = spike[0]

    top_load.wait()
    bottom_load.wait()
    terms = []
    for side, place in enumerate((0, CZ - 1)):
        link = (links[1, side, 0], links[1, side, 1])
        for table, r in ((top, 0), (bottom, 7)):
            for part in range(2):
                for c in range(NC):
                    lanes = 128 * side
                    zcorner[part, c : c + 1, :] = table[part, c, r : r + 1, lanes : lanes + 128]
            at = place % 128
            value = tuple(
                jnp.broadcast_to(zcorner[part][:, at : at + 1], (NC, 128)) for part in range(2)
            )
            terms.append(cmul(link, value))
    left, right = chain(NC, 8, terms)
    square[...] = jnp.zeros_like(square)
    for i, value in enumerate(left + right):
        zresponse[i] = value
        square[i : i + 1, :] = zresponse[i, pl.ds(mez, 1), :]
    turned = jnp.transpose(square[...])
    held = jnp.zeros((64, 2 * CZ), F32)
    for i in range(4):
        held = held + turned[0:64, i : i + 1] * zspike[i : i + 1, :]
    for h in range(2):
        high, low = split(held if h == 0 else pltpu.roll(held, 4, 0))
        zfix[h, 0:64, :] = high
        zfix[h, 64:128, :] = high
        zfix[h, 128:192, :] = low
        zfix[h, 192:256, :] = low

    blocks_load.wait()
    owners_load.wait()
    padded[...] = jnp.full_like(padded, -1.0)
    count = listed.shape[1]
    padded[0, :, 0:count] = listed[...].astype(F32)
    padded[1, :, 0:count] = owners[...].astype(F32)
    ids, names = (
        jnp.transpose(jnp.broadcast_to(padded[n, pl.ds(me, 1), :], (128, 128))) for n in range(2)
    )
    across = lax.broadcasted_iota(jnp.int32, (128, 128), 1)
    down = lax.broadcasted_iota(jnp.int32, (128, 128), 0)
    same = (names == padded[1, pl.ds(me, 1), :]) & (across < down)
    rank = jnp.sum(same.astype(F32), axis=1, keepdims=True)
    slot = jnp.where(names[:, 0:1] < 0.0, -1.0, CAP * names[:, 0:1] + rank)
    k = lax.broadcasted_iota(jnp.int32, (1, SLOT * NG), 1)
    hit = slot == (k // (2 * BY)).astype(F32)
    block = jnp.sum(jnp.where(hit, ids[:, 0:1] + 1.0, 0.0), axis=0, keepdims=True)
    onehot = rows_of(block)
    for n in range(SLOT * NG // 128):
        for m in range(2):
            pick[128 * n : 128 * n + 128, 128 * m : 128 * m + 128] = jnp.transpose(
                onehot[128 * m : 128 * m + 128, 128 * n : 128 * n + 128]
            ).astype(BF)

    pltpu.make_async_copy(
        values_in.at[pl.ds(0, UNITS - 1)], values_in.at[pl.ds(0, UNITS - 1)], value_sem.at[1]
    ).wait()

    for part, (first, last) in enumerate(PARTS):
        for p in range(first, last):
            for x in (2 * p, 2 * p + 1):
                for h in range(2):
                    v = values_in[2 * x + h]
                    lre, lim, rre, rim = (v[i : i + 1, :] for i in range(4))
                    re = solved[x, 0:CY, 128 * h : 128 * h + 128]
                    im = solved[x, CY:, 128 * h : 128 * h + 128]
                    re = re + (spikes[0] * lre - spikes[1] * lim)
                    re = re + (spikes[2] * rre - spikes[3] * rim)
                    im = im + (spikes[0] * lim + spikes[1] * lre)
                    im = im + (spikes[2] * rim + spikes[3] * rre)
                    for c, value in enumerate((re, im)):
                        high, low = split(value)
                        at = CZ * c + 128 * h
                        field[0, x, :, at : at + 128] = high
                        field[1, x, :, at : at + 128] = low
                found = dot3(zedge[0], zedge[1], field[0, x], field[1, x], NT)
                zheads[p, 4 * (x % 2) : 4 * (x % 2) + 4, :] = found[0:4, :]

        def send_zheads(s, carry):
            pltpu.make_async_remote_copy(
                src_ref=zheads.at[pl.ds(first, last - first)],
                dst_ref=zall.at[mez, pl.ds(first, last - first)],
                send_sem=z_send.at[part],
                recv_sem=z_recv.at[part],
                device_id={"gz": lax.rem(mez + s, NC)},
                device_id_type=MESH,
            ).start()
            return carry

        lax.fori_loop(1, NC, send_zheads, 0)
        for p in range(first, last):
            zall[mez, p] = zheads[p]

    stores = []
    for part, (first, last) in enumerate(PARTS):
        planes = pl.ds(2 * first, 2 * (last - first))
        for x in range(2 * first, 2 * last):
            solved[x, 0:CY, :] = dot3(
                field[0, x], field[1, x], zemb[0, 0:CZ, :], zemb[1, 0:CZ, :], NT
            )
            solved[x, CY:, :] = dot3(
                field[0, x], field[1, x], zemb[0, CZ:, :], zemb[1, CZ:, :], NT
            )
        if part == 0:
            absorber_load.wait()
        view = zall.at[pl.ds(0, NC - 1), pl.ds(first, last - first)]
        pltpu.make_async_copy(view, view, z_recv.at[part]).wait()
        for p in range(first, last):
            g = zall[:, p].reshape(8 * NC, 128)
            high = g.astype(BF).astype(F32)
            turned = jnp.transpose(jnp.concatenate([high, g - high], axis=0)).astype(BF)
            turned = jnp.concatenate([turned, turned], axis=1)
            folded = []
            for x in (2 * p, 2 * p + 1):
                fix = dot(turned, zfix[x % 2])
                kept = jnp.exp(-absorber[x])
                rows = []
                for c in range(2):
                    value = solved[x, CY * c : CY * c + CY, :] + fix[:, CZ * c : CZ * c + CZ]
                    left = value * kept
                    damped[c, x] = left
                    lost = value - left
                    rows.append(lost[:, 0:128] + lost[:, 128:256])
                folded.append(jnp.concatenate(rows, axis=0))
            high, low = split(jnp.concatenate(folded, axis=1))
            chosen = dot(pick[...], high) + dot(pick[...], low)
            for n in range(2):
                outgoing[2 * p + n] = chosen[:, 128 * n : 128 * n + 128].reshape(NG, SLOT, 128)

        def send_blocks(s, carry):
            peer = lax.rem(me + s, NG)
            pltpu.make_async_remote_copy(
                src_ref=outgoing.at[planes, peer],
                dst_ref=incoming.at[planes, me],
                send_sem=block_send.at[part],
                recv_sem=block_recv.at[part],
                device_id={"gy": peer},
                device_id_type=MESH,
            ).start()
            return carry

        lax.fori_loop(1, NG, send_blocks, 0)
        for x in range(2 * first, 2 * last):
            incoming[x, me] = outgoing[x, me]
        store = pltpu.make_async_copy(
            damped.at[:, planes], damped_hbm.at[:, planes], damped_sem.at[part]
        )
        store.start()
        stores.append(store)

    source = lax.broadcasted_iota(jnp.int32, (NG, SLOT * NG), 0)
    mine = (padded[1] == me.astype(F32)).astype(F32)
    rank = dot(mine.astype(BF), (down < across).astype(F32).astype(BF))
    total = jnp.zeros((NG, SLOT * NG), F32)
    for n in range(CAP):
        hit = jnp.where(rank == float(n), mine, 0.0)
        found = jnp.sum(hit * (padded[0] + 1.0), axis=1, keepdims=True)
        total = total + jnp.where((k // (2 * BY)) % CAP == n, found, 0.0)
    total = jnp.where(k // SLOT == source, total, 0.0)
    onehot = rows_of(jnp.sum(total, axis=0, keepdims=True)).astype(BF)
    tables_load.wait()
    for n in range(2):
        ytab[n] = dot(tables[n], onehot).astype(BF)
    phase_load.wait()
    norm = 1.0 / math.sqrt(CY * CZ)
    volkov[0] = jnp.cos(phase[...])
    volkov[1] = jnp.sin(phase[...])

    for part, (first, last) in enumerate(PARTS):
        planes = pl.ds(2 * first, 2 * (last - first))
        view = incoming.at[planes, pl.ds(0, NG - 1)]
        pltpu.make_async_copy(view, view, block_recv.at[part]).wait()
        for p in range(first, last):
            both = [incoming[2 * p + n].reshape(SLOT * NG, 128) for n in range(2)]
            high, low = split(jnp.concatenate(both, axis=1))
            along_y = dot3(ytab[0], ytab[1], high, low)
            lines = [
                jnp.concatenate(
                    [along_y[0:K, 128 * n : 128 * n + 128], along_y[K:, 128 * n : 128 * n + 128]],
                    axis=1,
                )
                for n in range(2)
            ]
            high, low = split(jnp.concatenate(lines, axis=0))
            both = dot3(high, low, tables[2], tables[3])
            for n in range(2):
                value = (both[K * n : K * n + K, 0:K], both[K * n : K * n + K, K:])
                re, im = cmul((volkov[0], volkov[1]), value)
                spectrum[0, 2 * p + n] = re * norm
                spectrum[1, 2 * p + n] = im * norm
        store = pltpu.make_async_copy(
            spectrum.at[:, planes], spectrum_hbm.at[:, planes], spectrum_sem.at[part]
        )
        store.start()
        stores.append(store)

    def sent(view, sem):
        pltpu.make_async_copy(view, view, sem).wait()

    sent(gathered.at[pl.ds(0, NG - 1)], head_sem.at[0])
    sent(values_in.at[pl.ds(0, UNITS - 1)], value_sem.at[0])
    for part, (first, last) in enumerate(PARTS):
        sent(zall.at[pl.ds(0, NC - 1), pl.ds(first, last - first)], z_send.at[part])
        planes = pl.ds(2 * first, 2 * (last - first))
        sent(outgoing.at[planes, pl.ds(0, NG - 1)], block_send.at[part])
    for store in stores:
        store.wait()


def phase_tables():
    n, k = np.arange(K)[:, None], np.arange(K)[None, :]
    angle = 2.0 * np.pi / K * ((n * k) % K) - np.pi * (n % 2)
    re, im = np.cos(angle), -np.sin(angle)
    along_y = np.block([[re.T, -im.T], [im.T, re.T]]).astype(np.float32)
    along_z = np.block([[re, im], [-im, re]]).astype(np.float32)
    found = []
    for table in (along_y, along_z):
        high = table.astype(BF)
        found += [high, (table - high.astype(np.float32)).astype(BF)]
    return np.stack(found)


def body(
    wavefunction,
    absorber,
    row_inverse,
    column_inverse,
    link_terms,
    shell_blocks,
    owner_map,
    volkov_phase,
):
    count = shell_blocks.shape[2]
    any_space = pl.BlockSpec(memory_space=pl.ANY)
    smem = pl.BlockSpec(memory_space=pltpu.SMEM)
    V = pltpu.VMEM
    dma = pltpu.SemaphoreType.DMA
    parts = len(PARTS)
    return pl.pallas_call(
        kernel,
        out_shape=(
            jax.ShapeDtypeStruct((2, NX, CY, CZ), F32),
            jax.ShapeDtypeStruct((2, NX, K, K), F32),
        ),
        in_specs=[smem] + [any_space] * 8,
        out_specs=(any_space, any_space),
        scratch_shapes=[
            V((2, NX, CY, CZ), F32),
            V((NX, CY, CZ), F32),
            V((2, CY, CY), F32),
            V((2, CZ, CZ), F32),
            V((2, NC, 8, CZ), F32),
            V((2, NC, 8, CZ), F32),
            V((NG, count), jnp.int32),
            V((NG, count), jnp.int32),
            V((K, K), F32),
            V((4, 2 * K, 2 * K), BF),
            V((2, 2 * CY, 2 * CY), BF),
            V((16, 2 * CY), F32),
            V((2, 16, 2 * CY), BF),
            V((4, CY, 128), F32),
            V((2, NX, 2 * CY, CZ), BF),
            V((UNITS, 5, 1, 128), F32),
            V((NG, 5, 1, 128), F32),
            V((NG, 128), F32),
            V((4 * NG, 128), F32),
            V((4 * NG, 128), F32),
            V((NG, 4, 128), F32),
            V((UNITS, 4, 128), F32),
            V((NX, 2 * CY, CZ), F32),
            V((2, NX, CY, 2 * CZ), BF),
            V((2, 2 * CZ, 2 * CZ), BF),
            V((16, 2 * CZ), F32),
            V((2, 16, 2 * CZ), BF),
            V((PAIRS, 8, 128), F32),
            V((NC, PAIRS, 8, 128), F32),
            V((2, NC, 128), F32),
            V((4, NC, 128), F32),
            V((128, 128), F32),
            V((4, 2 * CZ), F32),
            V((2, 256, 2 * CZ), BF),
            V((2, NG, 128), F32),
            V((SLOT * NG, 2 * K), BF),
            V((2, NX, CY, CZ), F32),
            V((NX, NG, SLOT, 128), F32),
            V((NX, NG, SLOT, 128), F32),
            V((2, 2 * K, SLOT * NG), BF),
            V((2, K, K), F32),
            V((2, NX, K, K), F32),
            dma((10,)),
            dma((parts,)),
            dma((parts,)),
            dma((2,)),
            dma((2,)),
            dma((parts,)),
            dma((parts,)),
            dma((parts,)),
            dma((parts,)),
        ],
        compiler_params=pltpu.CompilerParams(
            collective_id=0, has_side_effects=True, vmem_limit_bytes=48 * 1024 * 1024
        ),
    )(
        link_terms,
        wavefunction,
        absorber,
        row_inverse,
        column_inverse.reshape(2, NC, CZ, CZ),
        shell_blocks.reshape(NG, count),
        owner_map.reshape(NG, count),
        volkov_phase,
        phase_tables(),
    )


def solution(mesh):
    placed = (
        P(None, None, "gy", "gz"),
        P(None, "gy", "gz"),
        P(None, "gy", None),
        P(),
        P(),
        P("gz", None, None),
        P("gz", None, None, None),
        P(),
    )
    return jax.shard_map(
        body,
        mesh=mesh,
        in_specs=placed,
        out_specs=(P(None, None, "gy", "gz"), P(None, "gy", "gz", None)),
        check_vma=False,
    )
```

time: 97.6 us -> 86.1 us (0.88)
  Pallas kernels: 82.7 us -> 76 us
  other arithmetic: 5.19 us -> 0 us
    pallas_call x1, Pallas kernels: 82.7 us -> 76 us  [body(): pl.pallas_call(kernel, out_shape=(jax.ShapeDtypeStruct((2, NX, CY, CZ), F...]
    unnamed x10 -> x16, local copies, waits for them, and re-layouts: 6.31 us -> 8.41 us
    reduce_sum x3 -> x0, other arithmetic: 1.91 us -> none  [the longest x1 1.67 us: body(): jnp.sum(((targets[:, :, None] == targets[:, None, :]) & earlier[None]).as...]
    eq x2 -> x0, other arithmetic: 1.39 us -> none  [the longest x1 0.72 us: body(): targets == row_rank]
    another operation x1 -> x0, local copies, waits for them, and re-layouts: 1.08 us -> none  [body(): volkov = jnp.stack([jnp.cos(volkov_phase), jnp.sin(volkov_phase)])]
where the time goes in v1:
time: 86.1 us; the launch traced here: 85.1 us
  Pallas kernels  76 us (88%)
  local copies, waits for them, and re-layouts  8.41 us (10%)
    pallas_call x1, Pallas kernels, body(): pl.pallas_call(kernel, out_shape=(jax.ShapeDtypeStruct((2, NX, CY, CZ), F...  76 us
    unnamed x16, local copies, waits for them, and re-layouts  8.41 us

profile of v1, /device:TPU:24, one launch (start us, length us, event | category | flops | bytes accessed | tf_op | source)
XLA Modules:
  0.0 85.1 jit_solution(5982762819519508318)
XLA Ops:
  0.6 0.0 copy-start
  0.6 1.2 %copy-done = f32[8,128,256]{2,1,0:T(8,128)S(1)} copy-done((f32[8,128,256]{2,1,0:T(8,128)S(1)}, f32[8,128,256]{2,1,0:T(8,128)}, u32[]{:S(2)}) %copy-start) | copy-done | bytes 1048600
  1.9 0.0 copy-start.1
  1.9 1.0 %copy-done.1 = bf16[4,256,256]{2,1,0:T(8,128)(2,1)S(1)} copy-done((bf16[4,256,256]{2,1,0:T(8,128)(2,1)S(1)}, bf16[4,256,256]{2,1,0:T(8,128)(2,1)}, u32[]{:S(2)}) %copy-start.1) | copy-done | bytes 524312
  2.9 0.0 copy-start.2
  2.9 0.9 %copy-done.2 = f32[2,128,128]{2,1,0:T(8,128)S(1)} copy-done((f32[2,128,128]{2,1,0:T(8,128)S(1)}, f32[2,128,128]{2,1,0:T(8,128)}, u32[]{:S(2)}) %copy-start.2) | copy-done | bytes 131096
  3.8 0.0 copy-start.3
  3.8 0.8 copy-done.3
  4.6 0.0 copy-start.4
  4.6 0.7 copy-done.4
  5.4 0.0 copy-start.5
  5.4 0.7 copy-done.5
  6.1 0.0 copy-start.6
  6.1 0.7 copy-done.6
  6.8 76.0 %shard_map.104 = (f32[2,8,128,256]{3,2,1,0:T(8,128)S(1)}, f32[2,8,128,128]{3,2,1,0:T(8,128)S(1)}) custom-call(f32[2,2,2]{2,1,0:T(2,128)S(1)} %copy-done.6, f32[2,8,128,256]{3,2,1,0:T(8,128)} %wave_hbm.1, f32[8,128,256]{2,1,0:T(8,128)S(1)} %copy-done, f32[2,128,128]{2,1,0:T(8,128)S(1)} %copy-done.2, f32[2,8,256,256]{3,2,1,0:T(8,128)} %bitcast.5, ...), custom_call_target="tpu_custom_call" | custom-call | tf_op jit(solution)/shard_map/pallas_call | solution.py:574
  82.8 1.3 %copy.13 = f32[2,8,128,256]{3,2,1,0:T(8,128)} copy(f32[2,8,128,256]{3,2,1,0:T(8,128)S(1)} %get-tuple-element.4) | data formatting | bytes 4194304
  84.1 1.0 %copy.14 = f32[2,8,128,128]{3,2,1,0:T(8,128)} copy(f32[2,8,128,128]{3,2,1,0:T(8,128)S(1)} %get-tuple-element.5) | data formatting | bytes 2097152
Async XLA Ops:
  0.6 1.2 %copy-start = (f32[8,128,256]{2,1,0:T(8,128)S(1)}, f32[8,128,256]{2,1,0:T(8,128)}, u32[]{:S(2)}) copy-start(f32[8,128,256]{2,1,0:T(8,128)} %absorber_hbm.1) | copy-start | bytes 3145732
  1.9 1.0 %copy-start.1 = (bf16[4,256,256]{2,1,0:T(8,128)(2,1)S(1)}, bf16[4,256,256]{2,1,0:T(8,128)(2,1)}, u32[]{:S(2)}) copy-start(bf16[4,256,256]{2,1,0:T(8,128)(2,1)} %constant.2.clone.tables_hbm) | copy-start | bytes 1572868
  2.9 0.9 %copy-start.2 = (f32[2,128,128]{2,1,0:T(8,128)S(1)}, f32[2,128,128]{2,1,0:T(8,128)}, u32[]{:S(2)}) copy-start(f32[2,128,128]{2,1,0:T(8,128)} %row_hbm.1) | copy-start | bytes 393220
  3.8 0.8 copy-start.3
  4.6 0.7 copy-start.4
  5.4 0.7 copy-start.5
  6.1 0.7 copy-start.6

commit v2 on v1

--- a/solution.py
+++ b/solution.py
@@ -162,7 +162,9 @@
     psi,
     heads,
     gathered,
+    edge_line,
     edges,
+    edge_rows,
     flat_a,
     flat_v,
     values_out,
@@ -190,6 +192,7 @@
     load_sem,
     damped_sem,
     spectrum_sem,
+    edge_sem,
     head_sem,
     value_sem,
     z_send,
@@ -223,17 +226,17 @@
         return copy
 
     row_load = load(0, row_hbm, row)
-    wave_load = load(1, wave_hbm, wave)
+    wave_loads = [load(9 + x, wave_hbm.at[:, x], wave.at[:, x]) for x in range(NX)]
     lax.fori_loop(1, NG, greet, 0)
     lax.fori_loop(1, NC, greet_z, 0)
-    column_load = load(2, column_hbm.at[:, mez], column)
-    top_load = load(3, column_hbm.at[:, :, pl.ds(0, 8), :], top)
-    bottom_load = load(4, column_hbm.at[:, :, pl.ds(CZ - 8, 8), :], bottom)
-    blocks_load = load(5, blocks_hbm, listed)
-    owners_load = load(6, owners_hbm, owners)
-    absorber_load = load(7, absorber_hbm, absorber)
-    tables_load = load(8, tables_hbm, tables)
-    phase_load = load(9, phase_hbm, phase)
+    column_load = load(1, column_hbm.at[:, mez], column)
+    top_load = load(2, column_hbm.at[:, :, pl.ds(0, 8), :], top)
+    bottom_load = load(3, column_hbm.at[:, :, pl.ds(CZ - 8, 8), :], bottom)
+    blocks_load = load(4, blocks_hbm, listed)
+    owners_load = load(5, owners_hbm, owners)
+    absorber_load = load(6, absorber_hbm, absorber)
+    tables_load = load(7, tables_hbm, tables)
+    phase_load = load(8, phase_hbm, phase)
 
     row_load.wait()
     embed_edges(yedge, ywide, CY, row)
@@ -247,19 +250,31 @@
             for n, r in enumerate((0, CY - 1)):
                 term = spikes[2 * side + part, r : r + 1, :]
                 edge_row = jnp.where(lane == 4 * side + 2 * n + part, term, edge_row)
-    for u in range(UNITS):
-        heads[u, 4] = edge_row
-
-    wave_load.wait()
+    edge_line[0] = edge_row
+
     for x in range(NX):
+        wave_loads[x].wait()
         high, low = split(jnp.concatenate([wave[0, x], wave[1, x]], axis=0))
         psi[0, x], psi[1, x] = high, low
         found = dot3(yedge[0], yedge[1], high, low)
         for h in range(2):
-            for i in range(4):
-                heads[2 * x + h, i] = found[i : i + 1, 128 * h : 128 * h + 128]
+            heads[2 * x + h] = found[0:4, 128 * h : 128 * h + 128]
 
     pl.semaphore_wait(barrier, NG - 1 + NC - 1)
+
+    def send_edges(s, carry):
+        pltpu.make_async_remote_copy(
+            src_ref=edge_line,
+            dst_ref=edges.at[pl.ds(me, 1)],
+            send_sem=edge_sem.at[0],
+            recv_sem=edge_sem.at[1],
+            device_id={"gy": lax.rem(me + s, NG)},
+            device_id_type=MESH,
+        ).start()
+        return carry
+
+    lax.fori_loop(1, NG, send_edges, 0)
+    edges[me] = edge_row
 
     def send_heads(s, carry):
         peer = lax.rem(me + s, NG)
@@ -276,6 +291,15 @@
     lax.fori_loop(1, NG, send_heads, 0)
     gathered[me] = heads[unit]
 
+    pltpu.make_async_copy(
+        edges.at[pl.ds(0, NG - 1)], edges.at[pl.ds(0, NG - 1)], edge_sem.at[1]
+    ).wait()
+    for j in range(NG):
+        edge_rows[j : j + 1, :] = edges[j]
+    wide = [jnp.broadcast_to(edge_rows[:, i : i + 1], (NG, 128)) for i in range(8)]
+    left, right = chain(NG, 4, [(wide[i], wide[i + 1]) for i in (0, 2, 4, 6)])
+    for i, value in enumerate(left + right):
+        flat_a[pl.ds(i, NG, stride=4), :] = value
     embed(yemb, CY, row[0], row[1])
     for x in range(NX):
         solved[x] = dot3(yemb[0], yemb[1], psi[0, x], psi[1, x])
@@ -284,13 +308,7 @@
         gathered.at[pl.ds(0, NG - 1)], gathered.at[pl.ds(0, NG - 1)], head_sem.at[1]
     ).wait()
     for j in range(NG):
-        for i in range(4):
-            flat_v[4 * j + i : 4 * j + i + 1, :] = gathered[j, i]
-        edges[j : j + 1, :] = gathered[j, 4]
-    wide = [jnp.broadcast_to(edges[:, i : i + 1], (NG, 128)) for i in range(8)]
-    left, right = chain(NG, 4, [(wide[i], wide[i + 1]) for i in (0, 2, 4, 6)])
-    for i, value in enumerate(left + right):
-        flat_a[pl.ds(i, NG, stride=4), :] = value
+        flat_v[4 * j : 4 * j + 4, :] = gathered[j]
     ah, al = split(flat_a[...])
     vh, vl = split(flat_v[...])
     found = dot3(ah, al, vh, vl)
@@ -391,7 +409,8 @@
         values_in.at[pl.ds(0, UNITS - 1)], values_in.at[pl.ds(0, UNITS - 1)], value_sem.at[1]
     ).wait()
 
-    for part, (first, last) in enumerate(PARTS):
+    def meet_z(part):
+        first, last = PARTS[part]
         for p in range(first, last):
             for x in (2 * p, 2 * p + 1):
                 for h in range(2):
@@ -427,7 +446,10 @@
             zall[mez, p] = zheads[p]
 
     stores = []
+    meet_z(0)
     for part, (first, last) in enumerate(PARTS):
+        if part + 1 < len(PARTS):
+            meet_z(part + 1)
         planes = pl.ds(2 * first, 2 * (last - first))
         for x in range(2 * first, 2 * last):
             solved[x, 0:CY, :] = dot3(
@@ -532,6 +554,7 @@
     def sent(view, sem):
         pltpu.make_async_copy(view, view, sem).wait()
 
+    sent(edges.at[pl.ds(0, NG - 1)], edge_sem.at[0])
     sent(gathered.at[pl.ds(0, NG - 1)], head_sem.at[0])
     sent(values_in.at[pl.ds(0, UNITS - 1)], value_sem.at[0])
     for part, (first, last) in enumerate(PARTS):
@@ -577,7 +600,7 @@
             jax.ShapeDtypeStruct((2, NX, CY, CZ), F32),
             jax.ShapeDtypeStruct((2, NX, K, K), F32),
         ),
-        in_specs=[smem] + [any_space] * 8,
+        in_specs=[smem] + [pl.BlockSpec(memory_space=pltpu.HBM)] * 8,
         out_specs=(any_space, any_space),
         scratch_shapes=[
             V((2, NX, CY, CZ), F32),
@@ -595,8 +618,10 @@
             V((2, 16, 2 * CY), BF),
             V((4, CY, 128), F32),
             V((2, NX, 2 * CY, CZ), BF),
-            V((UNITS, 5, 1, 128), F32),
-            V((NG, 5, 1, 128), F32),
+            V((UNITS, 4, 128), F32),
+            V((NG, 4, 128), F32),
+            V((1, 1, 128), F32),
+            V((NG, 1, 128), F32),
             V((NG, 128), F32),
             V((4 * NG, 128), F32),
             V((4 * NG, 128), F32),
@@ -622,9 +647,10 @@
             V((2, 2 * K, SLOT * NG), BF),
             V((2, K, K), F32),
             V((2, NX, K, K), F32),
-            dma((10,)),
+            dma((9 + NX,)),
             dma((parts,)),
             dma((parts,)),
+            dma((2,)),
             dma((2,)),
             dma((2,)),
             dma((parts,)),
@@ -633,7 +659,7 @@
             dma((parts,)),
         ],
         compiler_params=pltpu.CompilerParams(
-            collective_id=0, has_side_effects=True, vmem_limit_bytes=48 * 1024 * 1024
+            collective_id=0, has_side_effects=True, vmem_limit_bytes=60 * 1024 * 1024
         ),
     )(
         link_terms,

time: 86.1 us -> 82.4 us (0.957)
  local copies, waits for them, and re-layouts: 8.41 us -> 4.16 us
  Pallas kernels: 76 us -> 76.9 us
    unnamed x16 -> x4, local copies, waits for them, and re-layouts: 8.41 us -> 4.16 us
    pallas_call x1, Pallas kernels: 76 us -> 76.9 us  [body(): pl.pallas_call(kernel, out_shape=(jax.ShapeDtypeStruct((2, NX, CY, CZ), F...]
where the time goes in v2:
time: 82.4 us; the launch traced here: 81.7 us
  Pallas kernels  76.9 us (93%)
  local copies, waits for them, and re-layouts  4.16 us (5%)
    pallas_call x1, Pallas kernels, body(): pl.pallas_call(kernel, out_shape=(jax.ShapeDtypeStruct((2, NX, CY, CZ), F...  76.9 us
    unnamed x4, local copies, waits for them, and re-layouts  4.16 us

profile of v2, /device:TPU:24, one launch (start us, length us, event | category | flops | bytes accessed | tf_op | source)
XLA Modules:
  0.0 81.7 jit_solution(3896977933308507955)
XLA Ops:
  0.6 76.9 %shard_map.104 = (f32[2,8,128,256]{3,2,1,0:T(8,128)}, f32[2,8,128,128]{3,2,1,0:T(8,128)}) custom-call(f32[2,2,2]{2,1,0:T(2,128)} %links.1, f32[2,8,128,256]{3,2,1,0:T(8,128)} %wave_hbm.1, f32[8,128,256]{2,1,0:T(8,128)} %absorber_hbm.1, f32[2,128,128]{2,1,0:T(8,128)} %row_hbm.1, f32[2,8,256,256]{3,2,1,0:T(8,128)} %bitcast.3, s32[32,56]{1,0:T(8,128)} %bitcast.4, ...), custom_call_target="tpu_custom_call" | custom-call | tf_op jit(solution)/shard_map/pallas_call | solution.py:597
  77.5 0.0 copy-start
  77.5 3.2 %copy.13 = f32[2,8,128,256]{3,2,1,0:T(8,128)} copy(f32[2,8,128,256]{3,2,1,0:T(8,128)} %get-tuple-element.4) | data formatting | bytes 4194304
  80.7 0.0 copy-done
  80.7 1.0 %copy.14 = f32[2,8,128,128]{3,2,1,0:T(8,128)} copy(f32[2,8,128,128]{3,2,1,0:T(8,128)S(1)} %copy-done) | data formatting | bytes 2097152
Async XLA Ops:
  77.5 3.2 %copy-start = (f32[2,8,128,128]{3,2,1,0:T(8,128)S(1)}, f32[2,8,128,128]{3,2,1,0:T(8,128)}, u32[]{:S(2)}) copy-start(f32[2,8,128,128]{3,2,1,0:T(8,128)} %get-tuple-element.5) | copy-start | bytes 3145732

commit v3 on v2

--- a/solution.py
+++ b/solution.py
@@ -565,6 +565,36 @@
         store.wait()
 
 
+def hand_over(damped, spectrum, damped_out, spectrum_out, held_d, held_s, load_sem, store_sem):
+    ways = []
+    for x in range(0, NX, 2):
+        for n in range(2):
+            ways.append((damped, held_d, damped_out, n, x))
+    for x in range(0, NX, 4):
+        for n in range(2):
+            ways.append((spectrum, held_s, spectrum_out, n, x))
+    loads, stores = [], []
+    for number, (source, held, target, n, x) in enumerate(ways):
+        planes = pl.ds(x, 2 if source is damped else 4)
+        loads.append(
+            pltpu.make_async_copy(
+                source.at[n, planes], held.at[n, planes], load_sem.at[number]
+            )
+        )
+        stores.append(
+            pltpu.make_async_copy(
+                held.at[n, planes], target.at[n, planes], store_sem.at[number]
+            )
+        )
+    for load in loads:
+        load.start()
+    for load, store in zip(loads, stores):
+        load.wait()
+        store.start()
+    for store in stores:
+        store.wait()
+
+
 def phase_tables():
     n, k = np.arange(K)[:, None], np.arange(K)[None, :]
     angle = 2.0 * np.pi / K * ((n * k) % K) - np.pi * (n % 2)
@@ -594,7 +624,7 @@
     V = pltpu.VMEM
     dma = pltpu.SemaphoreType.DMA
     parts = len(PARTS)
-    return pl.pallas_call(
+    found = pl.pallas_call(
         kernel,
         out_shape=(
             jax.ShapeDtypeStruct((2, NX, CY, CZ), F32),
@@ -672,6 +702,19 @@
         volkov_phase,
         phase_tables(),
     )
+    return pl.pallas_call(
+        hand_over,
+        out_shape=tuple(jax.ShapeDtypeStruct(value.shape, F32) for value in found),
+        in_specs=[any_space, any_space],
+        out_specs=(any_space, any_space),
+        scratch_shapes=[
+            V((2, NX, CY, CZ), F32),
+            V((2, NX, K, K), F32),
+            dma((12,)),
+            dma((12,)),
+        ],
+        compiler_params=pltpu.CompilerParams(vmem_limit_bytes=60 * 1024 * 1024),
+    )(*found)
 
 
 def solution(mesh):

time: 82.4 us -> 81.1 us (0.984)
  local copies, waits for them, and re-layouts: 4.16 us -> 0 us
  Pallas kernels: 76.9 us -> 79.7 us
    unnamed x4 -> x0, local copies, waits for them, and re-layouts: 4.16 us -> none
    pallas_call x0 -> x1, Pallas kernels: none -> 2.81 us  [body(): pl.pallas_call(hand_over, out_shape=tuple((jax.ShapeDtypeStruct(value.sha...]
where the time goes in v3:
time: 81.1 us; the launch traced here: 80.3 us
  Pallas kernels  79.7 us (98%)
    pallas_call x1, Pallas kernels, body(): pl.pallas_call(kernel, out_shape=(jax.ShapeDtypeStruct((2, NX, CY, CZ), F...  76.9 us
    pallas_call x1, Pallas kernels, body(): pl.pallas_call(hand_over, out_shape=tuple((jax.ShapeDtypeStruct(value.sha...  2.81 us

profile of v3, /device:TPU:24, one launch (start us, length us, event | category | flops | bytes accessed | tf_op | source)
XLA Modules:
  0.0 80.3 jit_solution(13171321763161037898)
XLA Ops:
  0.6 76.9 %shard_map.104 = (f32[2,8,128,256]{3,2,1,0:T(8,128)}, f32[2,8,128,128]{3,2,1,0:T(8,128)}) custom-call(f32[2,2,2]{2,1,0:T(2,128)} %links.1, f32[2,8,128,256]{3,2,1,0:T(8,128)} %wave_hbm.1, f32[8,128,256]{2,1,0:T(8,128)} %absorber_hbm.1, f32[2,128,128]{2,1,0:T(8,128)} %row_hbm.1, f32[2,8,256,256]{3,2,1,0:T(8,128)} %bitcast.3, s32[32,56]{1,0:T(8,128)} %bitcast.4, ...), custom_call_target="tpu_custom_call" | custom-call | tf_op jit(solution)/shard_map/pallas_call | solution.py:627
  77.5 2.8 %shard_map.105 = (f32[2,8,128,256]{3,2,1,0:T(8,128)}, f32[2,8,128,128]{3,2,1,0:T(8,128)}) custom-call(f32[2,8,128,256]{3,2,1,0:T(8,128)} %get-tuple-element.4.damped, f32[2,8,128,128]{3,2,1,0:T(8,128)} %get-tuple-element.5.spectrum), custom_call_target="tpu_custom_call" | custom-call | tf_op jit(solution)/shard_map/pallas_call | solution.py:705

commit v4 on v3

--- a/solution.py
+++ b/solution.py
@@ -273,7 +273,7 @@
         ).start()
         return carry
 
-    lax.fori_loop(1, NG, send_edges, 0)
+    lax.fori_loop(1, NG, send_edges, 0, unroll=True)
     edges[me] = edge_row
 
     def send_heads(s, carry):
@@ -288,7 +288,7 @@
         ).start()
         return carry
 
-    lax.fori_loop(1, NG, send_heads, 0)
+    lax.fori_loop(1, NG, send_heads, 0, unroll=True)
     gathered[me] = heads[unit]
 
     pltpu.make_async_copy(
@@ -327,7 +327,7 @@
         ).start()
         return carry
 
-    lax.fori_loop(1, UNITS, send_values, 0)
+    lax.fori_loop(1, UNITS, send_values, 0, unroll=True)
     values_in[unit] = values_out[me]
 
     column_load.wait()
@@ -441,7 +441,7 @@
             ).start()
             return carry
 
-        lax.fori_loop(1, NC, send_zheads, 0)
+        lax.fori_loop(1, NC, send_zheads, 0, unroll=True)
         for p in range(first, last):
             zall[mez, p] = zheads[p]
 

time: 81.1 us -> 80.9 us (level)
  no operation moved by 1% of the time
where the time goes in v4:
time: 80.9 us; the launch traced here: 80.3 us
  Pallas kernels  79.7 us (99%)
    pallas_call x1, Pallas kernels, body(): pl.pallas_call(kernel, out_shape=(jax.ShapeDtypeStruct((2, NX, CY, CZ), F...  76.9 us
    pallas_call x1, Pallas kernels, body(): pl.pallas_call(hand_over, out_shape=tuple((jax.ShapeDtypeStruct(value.sha...  2.81 us

profile of v4, /device:TPU:24, one launch (start us, length us, event | category | flops | bytes accessed | tf_op | source)
XLA Modules:
  0.0 80.3 jit_solution(6712011612900106117)
XLA Ops:
  0.6 76.9 %shard_map.104 = (f32[2,8,128,256]{3,2,1,0:T(8,128)}, f32[2,8,128,128]{3,2,1,0:T(8,128)}) custom-call(f32[2,2,2]{2,1,0:T(2,128)} %links.1, f32[2,8,128,256]{3,2,1,0:T(8,128)} %wave_hbm.1, f32[8,128,256]{2,1,0:T(8,128)} %absorber_hbm.1, f32[2,128,128]{2,1,0:T(8,128)} %row_hbm.1, f32[2,8,256,256]{3,2,1,0:T(8,128)} %bitcast.3, s32[32,56]{1,0:T(8,128)} %bitcast.4, ...), custom_call_target="tpu_custom_call" | custom-call | tf_op jit(solution)/shard_map/pallas_call | solution.py:627
  77.5 2.8 %shard_map.105 = (f32[2,8,128,256]{3,2,1,0:T(8,128)}, f32[2,8,128,128]{3,2,1,0:T(8,128)}) custom-call(f32[2,8,128,256]{3,2,1,0:T(8,128)} %get-tuple-element.4.damped, f32[2,8,128,128]{3,2,1,0:T(8,128)} %get-tuple-element.5.spectrum), custom_call_target="tpu_custom_call" | custom-call | tf_op jit(solution)/shard_map/pallas_call | solution.py:705
